TPU v7x, 32 devices: a whole 2x2x4 slice. The times are simulated.
32 devices in a mesh: row: 8 (over z, y), col: 4 (over x, core).
Axes of the slice: x: 2, y: 2, z: 4, core: 2. Of those that a mesh axis runs over, the one named last changes fastest.
Arguments:
- matrix: bfloat16 [6, 4096, 12, 2048], P(None, 'row', None, 'col'), may hold values from -6 to 6
- multiplier: bfloat16 [2, 512, 512], replicated
- checksum_weight: float32 [6, 4096], P(None, 'row')
Outputs:
- factored: bfloat16 [6, 4096, 12, 2048], P(None, 'row', None, 'col')
- group_checksum: float32 [8, 12, 2048], P('row', None, 'col')
- total_checksum: float32 [12, 2048], P(None, 'col')
All inputs are finite; a program needn't handle non-finite values.
Results may differ from a plain program's by a relative error of at most 0.0056.
Values may be sent and summed in bfloat16 or wider, within the bound.
A program may use at most 256 MiB of HBM per device.

v0:
```python
import jax
import jax.numpy as jnp
from jax import lax
from jax.sharding import PartitionSpec as P

ELIMINATION_STEPS = 2


def broadcast(block, axis, holder):
    block = jnp.where(lax.axis_index(axis) == holder, block, jnp.zeros_like(block))
    return lax.psum(block, axis)


def apply_update(target, left, right):
    product = jnp.dot(left, right, preferred_element_type=jnp.float32)
    return (target.astype(jnp.float32) - product).astype(jnp.bfloat16)


def local(matrix, multiplier, checksum_weight):
    highest_precision = lax.Precision.HIGHEST
    row_count, block_extent, col_count, _ = matrix.shape
    grid_rows = lax.axis_size("row")
    grid_cols = lax.axis_size("col")
    my_row = lax.axis_index("row")
    local_grid_column = lax.axis_index("col")
    block_tiles = matrix.reshape(row_count * block_extent, col_count * block_extent)
    row_holder = jnp.arange(row_count, dtype=jnp.int32) * grid_rows + my_row
    column_holder = jnp.arange(col_count, dtype=jnp.int32) * grid_cols + local_grid_column
    weights = checksum_weight.reshape(row_count * block_extent)
    checks = jnp.dot(
        weights, block_tiles, precision=highest_precision, preferred_element_type=jnp.float32
    )
    value_of_zero = jnp.zeros((), jnp.bfloat16)
    for eliminate_block in range(ELIMINATION_STEPS):
        row_retained = jnp.repeat(row_holder > eliminate_block, block_extent)[:, None]
        column_retained = jnp.repeat(column_holder > eliminate_block, block_extent)[None, :]
        lower_factor = jnp.dot(
            block_tiles[:, :block_extent],
            multiplier[eliminate_block],
            preferred_element_type=jnp.float32,
        ).astype(jnp.bfloat16)
        lower_factor = jnp.where(row_retained, lower_factor, value_of_zero)
        panel_lower_part = broadcast(lower_factor, "col", eliminate_block)
        pivot_row_band = broadcast(
            jnp.where(column_retained, block_tiles[:block_extent], value_of_zero),
            "row",
            eliminate_block,
        )
        summed = jnp.dot(
            weights,
            panel_lower_part,
            precision=highest_precision,
            preferred_element_type=jnp.float32,
        )
        checks = checks - jnp.dot(
            summed, pivot_row_band, precision=highest_precision, preferred_element_type=jnp.float32
        )
        holds_pivot_block = local_grid_column == eliminate_block
        updated = apply_update(block_tiles, panel_lower_part, pivot_row_band)
        leading = jnp.where(
            holds_pivot_block & row_retained, panel_lower_part, updated[:, :block_extent]
        )
        block_tiles = jnp.concatenate([leading, updated[:, block_extent:]], axis=1)
    total = lax.psum(checks, "row")
    return (
        block_tiles.reshape(matrix.shape),
        checks.reshape(1, col_count, block_extent),
        total.reshape(col_count, block_extent),
    )


def solution(mesh):
    in_specs = (P(None, "row", None, "col"), P(), P(None, "row"))
    out_specs = (P(None, "row", None, "col"), P("row", None, "col"), P(None, "col"))
    return jax.shard_map(local, mesh=mesh, in_specs=in_specs, out_specs=out_specs, check_vma=False)
```

profile of v0, /device:TPU:6, one launch (start us, length us, event | category | flops | bytes accessed | tf_op | source)
XLA Modules:
  0.0 922.6 jit_solution(12969371502234736212)
XLA Ops:
  7.2 0.0 all-reduce.5.cloned.1.call-start
  7.2 0.1 broadcast_in_dim.68
  7.3 38.7 %copy.9 = bf16[6,512,12,512]{3,2,1,0:T(8,128)(2,1)} copy(bf16[6,512,12,512]{3,1,2,0:T(8,128)(2,1)} %param.3) | data formatting | bytes 75497472 | tf_op args[0]
  46.0 32.3 %copy.14 = bf16[384,8,12,512]{3,1,2,0:T(8,128)(2,1)} copy(bf16[384,8,12,512]{3,2,1,0:T(8,128)(2,1)} %bitcast.39) | data formatting | bytes 75497472
  78.4 0.0 copy-done.6
  78.4 5.3 fusion.4
  83.7 0.0 all-reduce.5.cloned.1.call-update
  83.7 0.0 all-reduce.7.cloned.1.call-start
  83.8 5.8 slice.32
  89.6 0.1 broadcast_in_dim.72
  89.7 8.4 copy.13
  98.1 8.7 copy.11
  106.8 6.1 select_select_fusion
  112.9 0.0 all-reduce.7.cloned.1.call-update
  113.0 0.2 all-reduce.9.cloned.1.call-start
  113.2 0.1 broadcast_in_dim.65
  113.3 39.4 %all-reduce.5.cloned.1.call-done = bf16[3072,512]{1,0:T(8,128)(2,1)} async-done(((bf16[3072,512]{1,0:T(8,128)(2,1)}), bf16[3072,512]{1,0:T(8,128)(2,1)}) %all-reduce.5.cloned.1.call-update) | async-done | bytes 3145744 | tf_op jit(solution)/shard_map/psum | solution.py:11
  152.7 215.0 %all-reduce.7.cloned.1.call-done = bf16[512,6144]{1,0:T(8,128)(2,1)} async-done(((bf16[512,6144]{1,0:T(8,128)(2,1)}), bf16[512,6144]{1,0:T(8,128)(2,1)}) %all-reduce.7.cloned.1.call-update) | async-done | bytes 6291472 | tf_op jit(solution)/shard_map/psum | solution.py:11
  367.7 37.3 %subtract_convert_fusion.1 = bf16[3072,6144]{1,0:T(8,128)(2,1)} fusion(bf16[3072,6144]{1,0:T(8,128)(2,1)} %bitcast.41, bf16[3072,512]{1,0:T(8,128)(2,1)} %all-reduce.5.cloned.1.call-done, bf16[512,6144]{1,0:T(8,128)(2,1)} %all-reduce.7.cloned.1.call-done), kind=kOutput, calls=%fused_computation.1 | convolution fusion | flops 19383975936 | bytes 84934656 | tf_op jit(solution)/shard_map/dot_general | solution.py:15
  405.0 0.0 copy-done
  405.0 3.1 slice_select_fusion.1
  408.1 1.6 copy-done.2
  409.8 3.7 fusion.6
  413.4 0.0 all-reduce.9.cloned.1.call-update
  413.5 0.3 all-reduce.11.cloned.1.call-start
  413.7 0.1 broadcast_in_dim.76
  413.8 23.4 %slice.42 = bf16[3072,5632]{1,0:T(8,128)(2,1)} slice(bf16[3072,6144]{1,0:T(8,128)(2,1)} %subtract_convert_fusion.1), slice={[0:3072], [512:6144]} | slice | bytes 69206016 | tf_op jit(solution)/shard_map/slice | solution.py:63
  437.2 7.4 fusion.2
  444.6 0.0 all-reduce.11.cloned.1.call-update
  444.6 0.7 copy-done.5
  445.4 19.3 %fusion.16 = f32[1,6144]{1,0:T(1,128)S(1)} fusion(f32[3072,1]{0,1:T(1,128)S(1)} %bitcast.44, bf16[3072,6144]{1,0:T(8,128)(2,1)} %bitcast.42), kind=kOutput, calls=%fused_computation.34 | convolution fusion | flops 226492416 | bytes 37785600 | tf_op jit(solution)/shard_map/dot_general | solution.py:30
  464.6 1.3 convolution_bitcast_fusion.1
  465.9 5.5 fusion.17
  471.5 8.8 all-reduce.9.cloned.1.call-done
  480.3 3.2 convolution_bitcast_fusion
  483.5 211.7 %all-reduce.11.cloned.1.call-done = bf16[512,6144]{1,0:T(8,128)(2,1)} async-done(((bf16[512,6144]{1,0:T(8,128)(2,1)}), bf16[512,6144]{1,0:T(8,128)(2,1)}) %all-reduce.11.cloned.1.call-update) | async-done | bytes 6291472 | tf_op jit(solution)/shard_map/psum | solution.py:11
  695.2 0.0 copy-done.3
  695.2 35.9 %subtract_convert_fusion = bf16[3072,6144]{1,0:T(8,128)(2,1)} fusion(bf16[3072,512]{1,0:T(8,128)(2,1)S(1)} %copy-done.3, bf16[3072,512]{1,0:T(8,128)(2,1)} %all-reduce.9.cloned.1.call-done, bf16[512,6144]{1,0:T(8,128)(2,1)} %all-reduce.11.cloned.1.call-done, bf16[3072,5632]{1,0:T(8,128)(2,1)} %slice.42), kind=kOutput, calls=%fused_computation | convolution fusion | flops 19440599040 | bytes 84934656 | tf_op jit(solution)/shard_map/dot_general | solution.py:15
  731.0 23.7 %slice.46 = bf16[3072,5632]{1,0:T(8,128)(2,1)} slice(bf16[3072,6144]{1,0:T(8,128)(2,1)} %subtract_convert_fusion), slice={[0:3072], [512:6144]} | slice | bytes 69206016 | tf_op jit(solution)/shard_map/slice | solution.py:63
  754.7 5.5 fusion.18
  760.2 0.0 copy-start.4
  760.3 31.3 %psum.39 = f32[12,512]{1,0:T(8,128)} all-reduce(f32[12,512]{1,0:T(8,128)S(1)} %reshape.44), channel_id=1, replica_groups=mesh['row'=8,'col'=4] {'row'}, use_global_device_ids=true, to_apply=%region_4.5 | all-reduce | flops 6144 | bytes 49152 | tf_op jit(solution)/shard_map/psum | solution.py:64
  791.6 0.0 copy-done.1
  791.6 4.2 slice_select_fusion
  795.8 24.9 %pad_maximum_fusion.1 = bf16[3072,6144]{1,0:T(8,128)(2,1)} fusion(bf16[3072,5632]{1,0:T(8,128)(2,1)} %slice.46, bf16[3072,512]{1,0:T(8,128)(2,1)} %slice_select_fusion), kind=kLoop, calls=%fused_computation.4 | loop fusion | flops 75497472 | bytes 75497472 | tf_op jit(solution)/shard_map/concatenate | solution.py:63
  820.6 0.0 copy-done.4
  820.6 65.1 %reshape.41 = bf16[6,512,12,512]{3,2,1,0:T(8,128)(2,1)} reshape(bf16[3072,6144]{1,0:T(8,128)(2,1)} %pad_maximum_fusion.1) | data formatting | bytes 75497472 | tf_op jit(solution)/shard_map/reshape | solution.py:66
  885.8 30.3 %copy.12 = bf16[6,512,12,512]{3,1,2,0:T(8,128)(2,1)} copy(bf16[6,512,12,512]{3,2,1,0:T(8,128)(2,1)} %reshape.41) | data formatting | bytes 75497472
  (21 shorter events, 0.2 us)
Async XLA Ops:
  7.2 145.5 %all-reduce.5.cloned.1.call-start = ((), (), s32[]{:S(2)}) async-start(), calls=%async_computation | async-start | bytes 6291456 | tf_op jit(solution)/shard_map/psum | solution.py:11
  46.0 32.3 %copy-start.6 = (bf16[2,512,512]{2,1,0:T(8,128)(2,1)S(1)}, bf16[2,512,512]{2,1,0:T(8,128)(2,1)}, u32[]{:S(2)}) copy-start(bf16[2,512,512]{2,1,0:T(8,128)(2,1)} %param.4) | copy-start | bytes 3145732
  83.7 284.0 %all-reduce.7.cloned.1.call-start = ((), (), s32[]{:S(2)}) async-start(), calls=%async_computation.1 | async-start | bytes 12582912 | tf_op jit(solution)/shard_map/psum | solution.py:11
  113.0 367.3 %all-reduce.9.cloned.1.call-start = ((), (), s32[]{:S(2)}) async-start(), calls=%async_computation.2 | async-start | bytes 6291456 | tf_op jit(solution)/shard_map/psum | solution.py:11
  152.7 252.3 %copy-start = (bf16[3072,512]{1,0:T(8,128)(2,1)S(1)}, bf16[3072,512]{1,0:T(8,128)(2,1)}, u32[]{:S(2)}) copy-start(bf16[3072,512]{1,0:T(8,128)(2,1)} %all-reduce.5.cloned.1.call-done) | copy-start | bytes 9437188
  405.0 4.7 copy-start.7
  408.1 1.7 copy-start.2
  413.5 281.7 %all-reduce.11.cloned.1.call-start = ((), (), s32[]{:S(2)}) async-start(), calls=%async_computation.3 | async-start | bytes 12582912 | tf_op jit(solution)/shard_map/psum | solution.py:11
  444.6 0.7 copy-start.5
  465.9 229.2 %copy-start.3 = (bf16[3072,512]{1,0:T(8,128)(2,1)S(1)}, bf16[3072,512]{1,0:T(8,128)(2,1)}, u32[]{:S(2)}) copy-start(bf16[3072,512]{1,0:T(8,128)(2,1)} %copy-done.2) | copy-start | bytes 9437188
  754.7 36.9 %copy-start.1 = (bf16[3072,512]{1,0:T(8,128)(2,1)S(1)}, bf16[3072,512]{1,0:T(8,128)(2,1)}, u32[]{:S(2)}) copy-start(bf16[3072,512]{1,0:T(8,128)(2,1)} %all-reduce.9.cloned.1.call-done) | copy-start | bytes 9437188
  760.2 60.4 %copy-start.4 = (f32[6144]{0:T(1024)}, f32[6144]{0:T(1024)S(1)}, u32[]{:S(2)}) copy-start(f32[6144]{0:T(1024)S(1)} %subtract_subtract_fusion) | copy-start | bytes 73732
Sparse Core Ops, SparseCore 0:
  83.8 68.7 all-reduce.4
  156.5 211.1 all-reduce.6
  413.6 66.6 all-reduce.8
  483.9 211.1 all-reduce.10
where the time goes:
time: 931 us; the launch traced here: 923 us
  waiting for transfers between devices  475 us (51%)
  local copies, waits for them, and re-layouts  239 us (26%)
  matrix products  117 us (13%)
  other arithmetic  45.7 us (5%)
  blocking collectives  31.3 us (3%)
  between operations  13.9 us (1%)
    psum x4, waiting for transfers between devices, broadcast(): return lax.psum(block, axis)  475 us
    unnamed x21, local copies, waits for them, and re-layouts  112 us
    dot_general x2, matrix products, apply_update(): product = jnp.dot(left, right, preferred_element_type=jnp.float32)  73.2 us
    reshape x1, local copies, waits for them, and re-layouts, local(): block_tiles.reshape(matrix.shape)  65.1 us
    slice x2, local copies, waits for them, and re-layouts, local(): block_tiles = jnp.concatenate([leading, updated[:, block_extent:]], axis=1)  47.1 us
    psum x1, blocking collectives, local(): total = lax.psum(checks, 'row')  31.3 us
    concatenate x1, other arithmetic, local(): block_tiles = jnp.concatenate([leading, updated[:, block_extent:]], axis=1)  24.9 us
    dot_general x1, matrix products, local(): jnp.dot(weights, block_tiles, precision=highest_precision, preferred_elem...  19.3 us
  transfers between devices with their start and end apart: 4, of which 4 were waited for; matrix products, arithmetic and copies ran while one was open for 10% of the time, Pallas kernels for 0%

commit v1 on v0

v1 whole, which is shorter than its diff:
```python
import functools

import jax
import jax.numpy as jnp
from jax import lax
from jax.experimental import pallas as pl
from jax.experimental.pallas import tpu as pltpu
from jax.sharding import PartitionSpec as P

SUBS = 4
MESH = pl.DeviceIdType.MESH


def kernel(dims, mt, mult, g, out, group, total, ubuf, lraw, lcat, ebuf, lzb, ucat, min_, mout,
           gcol, csum, crow, cbuf, usem, uzs, uys, lsem, lxs, lks, esem, ezs, eys, eks,
           insem, outsem, csend, crecv):
    grid_rows, grid_cols, row_blocks, col_blocks, size = dims
    f32, bf16 = jnp.float32, jnp.bfloat16
    sub, half = size // SUBS, size // 2
    me_r, me_c = lax.axis_index("row"), lax.axis_index("col")
    z, y, x, k = me_r // 2, me_r % 2, me_c // 2, me_c % 2
    depth_z, depth_x = grid_rows // 2, grid_cols // 2
    up, across = me_r + 2, me_r + 1 - 2 * y
    beyond, sibling = me_c + 2, me_c + 1 - 2 * k
    n_sub, n_unit = SUBS * col_blocks, 2 * col_blocks

    def remote(ref, send, recv, axis, to):
        return pltpu.make_async_remote_copy(
            src_ref=ref, dst_ref=ref, send_sem=send, recv_sem=recv,
            device_id={axis: to}, device_id_type=MESH)

    def u_rows(t):
        return pl.ds(pl.multiple_of((t % SUBS) * sub, sub), sub)

    def u_ref(band, t):
        return ubuf.at[band, t // SUBS, u_rows(t), :]

    def u_load(t):
        return pltpu.make_async_copy(mt.at[0, t // SUBS, u_rows(t), :], u_ref(y, t), usem.at[y, t])

    def u_up(t):
        return remote(u_ref(y, t), uzs.at[t], usem.at[y, t], "row", up)

    def u_across(t):
        return remote(u_ref(y, t), uys.at[t], usem.at[y, t], "row", across)

    def u_other(t):
        return remote(u_ref(1 - y, t), uys.at[t], usem.at[1 - y, t], "row", across)

    def relay_u(t):
        @pl.when(z == 0)
        def _():
            u_load(t).wait()

        @pl.when(z > 0)
        def _():
            u_up(t).wait_recv()

        @pl.when(z < depth_z - 1)
        def _():
            u_up(t).start()

        u_across(t).start()

    def l_load(a):
        return pltpu.make_async_copy(mt.at[a, 0], lraw.at[k, a], lsem.at[k, a])

    def l_beyond(a):
        return remote(lraw.at[k, a], lxs.at[a], lsem.at[k, a], "col", beyond)

    def l_sibling(a):
        return remote(lraw.at[k, a], lks.at[a], lsem.at[k, a], "col", sibling)

    def l_other(a):
        return remote(lraw.at[1 - k, a], lks.at[a], lsem.at[1 - k, a], "col", sibling)

    def relay_l(a):
        @pl.when(x == 0)
        def _():
            l_load(a).wait()

        @pl.when(x > 0)
        def _():
            l_beyond(a).wait_recv()

        @pl.when(x < depth_x - 1)
        def _():
            l_beyond(a).start()

        l_sibling(a).start()

    def e_local():
        rows = pl.ds(pl.multiple_of(k * half, half), half)
        return pltpu.make_async_copy(lraw.at[1 - y, 0, rows, :], ebuf.at[y, k], esem.at[y, k])

    def e_up():
        return remote(ebuf.at[y, k], ezs.at[0], esem.at[y, k], "row", up)

    def e_across():
        return remote(ebuf.at[y, k], eys.at[0], esem.at[y, k], "row", across)

    def e_other():
        return remote(ebuf.at[1 - y, k], eys.at[0], esem.at[1 - y, k], "row", across)

    def e_sibling(lane):
        return remote(ebuf.at[lane, k], eks.at[lane], esem.at[lane, k], "col", sibling)

    def e_from_sibling(lane):
        return remote(ebuf.at[lane, 1 - k], eks.at[lane], esem.at[lane, 1 - k], "col", sibling)

    def relay_e():
        l_other(0).wait_recv()

        @pl.when(z == 0)
        def _():
            e_local().start()
            e_local().wait()

        @pl.when(z > 0)
        def _():
            e_up().wait_recv()

        @pl.when(z < depth_z - 1)
        def _():
            e_up().start()

        e_across().start()

    def unit_slice(ref, u):
        return ref.at[:, u // 2, pl.ds(pl.multiple_of((u % 2) * half, half), half), :]

    def unit_in(u):
        return pltpu.make_async_copy(unit_slice(mt, u), min_.at[u % 2], insem.at[u % 2])

    def unit_out(u):
        return pltpu.make_async_copy(mout.at[u % 2], unit_slice(out, u), outsem.at[u % 2])

    @pl.when(z == 0)
    def _():
        @pl.loop(0, n_sub)
        def _(t):
            u_load(t).start()

    @pl.when(x == 0)
    def _():
        for a in range(row_blocks):
            l_load(a).start()

    unit_in(0).start()
    unit_in(1).start()

    barrier = pltpu.get_barrier_semaphore()
    for d in range(1, grid_rows):
        pl.semaphore_signal(barrier, inc=1, device_id={"row": (me_r + d) % grid_rows},
                            device_id_type=MESH)
    for d in range(1, grid_cols):
        pl.semaphore_signal(barrier, inc=1, device_id={"col": (me_c + d) % grid_cols},
                            device_id_type=MESH)
    pl.semaphore_wait(barrier, grid_rows + grid_cols - 2)

    ahead = n_sub - n_unit
    l_steps = [a * ahead // row_blocks for a in range(row_blocks)]
    for t in range(ahead):
        relay_u(t)
        for a in range(row_blocks):
            if l_steps[a] == t:
                relay_l(a)
        if t == 5 * ahead // 12:
            relay_e()
        if t == 7 * ahead // 12:
            e_sibling(y).start()
            e_other().wait_recv()
            e_sibling(1 - y).start()
        if t < row_blocks:
            gcol[t] = jnp.broadcast_to(g[t:t + 1, :], (128, size)).T

    for lane in range(2):
        e_from_sibling(lane).wait_recv()
    zero = jnp.zeros((), bf16)
    upper = ebuf[0].reshape(size, size)
    lzb[...] = jnp.dot(ebuf[1].reshape(size, size), mult[0],
                       preferred_element_type=f32).astype(bf16)

    @pl.loop(1, row_blocks)
    def _(a):
        l_other(a).wait_recv()

    @pl.loop(0, row_blocks)
    def _(a):
        block_row = a * grid_rows + me_r
        first = jnp.dot(lraw[0, a], mult[0], preferred_element_type=f32).astype(bf16)
        first = jnp.where(block_row > 0, first, zero)
        lcat[a, :, :size] = first
        product = jnp.dot(first, ebuf[0].reshape(size, size), preferred_element_type=f32)
        column = (lraw[1, a].astype(f32) - product).astype(bf16)
        second = jnp.dot(column, mult[1], preferred_element_type=f32).astype(bf16)
        lcat[a, :, size:] = jnp.where(block_row > 1, second, zero)

    def compute(u):
        m, h, slot = u // 2, u % 2, u % 2
        block_col = m * grid_cols + me_c

        @pl.when(h == 0)
        def _():
            for s in range(SUBS):
                u_other(m * SUBS + s).wait_recv()
            first = jnp.where(block_col > 0, ubuf[0, m], zero)
            ucat[:size, :] = first
            product = jnp.dot(lzb[...], first, preferred_element_type=f32)
            second = (ubuf[1, m].astype(f32) - product).astype(bf16)
            ucat[size:, :] = jnp.where(block_col > 1, second, zero)
            csum[...] = jnp.zeros_like(csum)

        unit_in(u).wait()

        @pl.when(u >= 2)
        def _():
            unit_out(u - 2).wait()

        rows = pl.ds(pl.multiple_of(h * half, half), half)

        @pl.loop(0, row_blocks)
        def _(a):
            product = jnp.dot(lcat[a, rows, :], ucat[...], preferred_element_type=f32)
            result = min_[slot, a].astype(f32) - product
            mout[slot, a] = result.astype(bf16)
            weight = gcol[a, rows, :]
            weight = jnp.concatenate([weight] * (size // 128), axis=1)
            csum[...] += jnp.sum((weight * result).reshape(half // 8, 8, size), axis=0)

        for band in range(2):
            @pl.when(block_col == band)
            def _():
                @pl.loop(0, row_blocks)
                def _(a):
                    @pl.when(a * grid_rows + me_r > band)
                    def _():
                        mout[slot, a] = lcat[a, rows, band * size:(band + 1) * size]

        unit_out(u).start()

        @pl.when(u + 2 < n_unit)
        def _():
            unit_in(u + 2).start()

        @pl.when(h == 1)
        def _():
            crow[pl.ds(m, 1), :] = jnp.sum(csum[...], axis=0, keepdims=True)

    @pl.loop(ahead, n_sub + 2)
    def _(t):
        @pl.when(t < n_sub)
        def _():
            relay_u(t)

        @pl.when(t >= ahead + 2)
        def _():
            compute(t - ahead - 2)

    cbuf[me_r] = crow[...]
    group[...] = crow[...]

    def c_copy(d, slot, to):
        return pltpu.make_async_remote_copy(
            src_ref=crow, dst_ref=cbuf.at[slot], send_sem=csend.at[d], recv_sem=crecv.at[d],
            device_id={"row": to}, device_id_type=MESH)

    unit_out(n_unit - 2).wait()
    for d in range(1, grid_rows):
        c_copy(d - 1, me_r, (me_r + d) % grid_rows).start()

    @pl.loop(0, n_sub)
    def _(t):
        @pl.when(z < depth_z - 1)
        def _():
            u_up(t).wait_send()

        u_across(t).wait_send()

    for a in range(row_blocks):
        @pl.when(x < depth_x - 1)
        def _():
            l_beyond(a).wait_send()

        l_sibling(a).wait_send()

    @pl.when(z < depth_z - 1)
    def _():
        e_up().wait_send()

    e_across().wait_send()
    for lane in range(2):
        e_sibling(lane).wait_send()
    unit_out(n_unit - 1).wait()
    for d in range(1, grid_rows):
        origin = (me_r + grid_rows - d) % grid_rows
        c_copy(d - 1, origin, (me_r + d) % grid_rows).wait_recv()
        c_copy(d - 1, me_r, (me_r + d) % grid_rows).wait_send()
    summed = cbuf[0]
    for r in range(1, grid_rows):
        summed = summed + cbuf[r]
    total[...] = summed


def local(matrix, multiplier, checksum_weight):
    row_blocks, size, col_blocks, _ = matrix.shape
    grid_rows, grid_cols = lax.axis_size("row"), lax.axis_size("col")
    dims = (grid_rows, grid_cols, row_blocks, col_blocks, size)
    bf16, f32 = jnp.bfloat16, jnp.float32
    half, n_sub = size // 2, SUBS * col_blocks
    dma = pltpu.SemaphoreType.DMA
    vmem = pl.BlockSpec(memory_space=pltpu.VMEM)
    hbm = pl.BlockSpec(memory_space=pltpu.HBM)
    tiles = matrix.transpose(0, 2, 1, 3)
    out, group, total = pl.pallas_call(
        functools.partial(kernel, dims),
        out_shape=(
            jax.ShapeDtypeStruct(tiles.shape, bf16),
            jax.ShapeDtypeStruct((col_blocks, size), f32),
            jax.ShapeDtypeStruct((col_blocks, size), f32),
        ),
        in_specs=[hbm, vmem, vmem],
        out_specs=(hbm, vmem, vmem),
        scratch_shapes=[
            pltpu.VMEM((2, col_blocks, size, size), bf16),
            pltpu.VMEM((2, row_blocks, size, size), bf16),
            pltpu.VMEM((row_blocks, size, 2 * size), bf16),
            pltpu.VMEM((2, 2, half, size), bf16),
            pltpu.VMEM((size, size), bf16),
            pltpu.VMEM((2 * size, size), bf16),
            pltpu.VMEM((2, row_blocks, half, size), bf16),
            pltpu.VMEM((2, row_blocks, half, size), bf16),
            pltpu.VMEM((row_blocks, size, 128), f32),
            pltpu.VMEM((8, size), f32),
            pltpu.VMEM((col_blocks, size), f32),
            pltpu.VMEM((grid_rows, col_blocks, size), f32),
            dma((2, n_sub)), dma((n_sub,)), dma((n_sub,)),
            dma((2, row_blocks)), dma((row_blocks,)), dma((row_blocks,)),
            dma((2, 2)), dma((1,)), dma((1,)), dma((2,)),
            dma((2,)), dma((2,)),
            dma((grid_rows - 1,)), dma((grid_rows - 1,)),
        ],
        compiler_params=pltpu.CompilerParams(
            collective_id=0, has_side_effects=True, vmem_limit_bytes=60 * 1024 * 1024),
    )(tiles, multiplier, checksum_weight)
    return (out.transpose(0, 2, 1, 3), group.reshape(1, col_blocks, size), total)


def solution(mesh):
    in_specs = (P(None, "row", None, "col"), P(), P(None, "row"))
    out_specs = (P(None, "row", None, "col"), P("row", None, "col"), P(None, "col"))
    return jax.shard_map(local, mesh=mesh, in_specs=in_specs, out_specs=out_specs, check_vma=False)
```

time: 931 us -> 222 us (0.24)
  waiting for transfers between devices: 475 us -> 0 us
  local copies, waits for them, and re-layouts: 239 us -> 27.4 us
  Pallas kernels: 0 us -> 194 us
  matrix products: 117 us -> 0 us
  other arithmetic: 45.7 us -> 0 us
  blocking collectives: 31.3 us -> 0 us
  between operations: 13.9 us -> 0.64 us
    psum x4 -> x0, waiting for transfers between devices: 475 us -> none  [broadcast(): return lax.psum(block, axis)]
    pallas_call x0 -> x1, Pallas kernels: none -> 194 us  [local(): pl.pallas_call(functools.partial(kernel, dims), out_shape=(jax.ShapeDtype...]
    dot_general x9 -> x0, matrix products: 117 us -> none  [the longest x2 73.2 us: apply_update(): product = jnp.dot(left, right, preferred_element_type=jnp.float32)]
    unnamed x21 -> x5, local copies, waits for them, and re-layouts: 112 us -> 27.4 us
    reshape x2 -> x0, local copies, waits for them, and re-layouts: 65.1 us -> none  [the longest x1 65.1 us: local(): block_tiles.reshape(matrix.shape)]
    slice x4 -> x0, local copies, waits for them, and re-layouts: 61.6 us -> none  [the longest x2 47.1 us: local(): block_tiles = jnp.concatenate([leading, updated[:, block_extent:]], axis=1)]
    psum x1 -> x0, blocking collectives: 31.3 us -> none  [local(): total = lax.psum(checks, 'row')]
    concatenate x1 -> x0, other arithmetic: 24.9 us -> none  [local(): block_tiles = jnp.concatenate([leading, updated[:, block_extent:]], axis=1)]
  transfers between devices with their start and end apart: 4 -> 0, of which waited for: 4 -> 0; matrix products, arithmetic and copies ran while one was open for 10% -> 0% of each run, Pallas kernels for 0% -> 0%
where the time goes in v1:
time: 222 us
  Pallas kernels  194 us (87%)
  local copies, waits for them, and re-layouts  27.4 us (12%)
    pallas_call x1, Pallas kernels, local(): pl.pallas_call(functools.partial(kernel, dims), out_shape=(jax.ShapeDtype...  194 us
    unnamed x5, local copies, waits for them, and re-layouts  27.4 us

profile of v1, /device:TPU:6, one launch (start us, length us, event | category | flops | bytes accessed | tf_op | source)
XLA Modules:
  0.0 222.2 jit_solution(7911839137205905696)
XLA Ops:
  0.6 194.2 %shard_map.58 = (bf16[6,12,512,512]{3,2,1,0:T(8,128)(2,1)}, f32[12,512]{1,0:T(8,128)}, f32[12,512]{1,0:T(8,128)}) custom-call(bf16[6,12,512,512]{3,2,1,0:T(8,128)(2,1)} %bitcast.3, bf16[2,512,512]{2,1,0:T(8,128)(2,1)} %mult.1, f32[6,512]{1,0:T(8,128)} %g.1), custom_call_target="tpu_custom_call" | custom-call | tf_op jit(solution)/shard_map/pallas_call | solution.py:315
  194.8 1.4 copy.6
  196.2 0.0 copy-start
  196.2 25.4 %copy.9 = bf16[6,512,12,512]{3,1,2,0:T(8,128)(2,1)} copy(bf16[6,512,12,512]{3,1,2,0:T(8,128)(2,1)} %bitcast.4) | data formatting | bytes 75497472
  221.6 0.0 copy-done
  221.6 0.6 copy.10
Async XLA Ops:
  196.2 25.4 %copy-start = (f32[12,512]{1,0:T(8,128)S(1)}, f32[12,512]{1,0:T(8,128)}, u32[]{:S(2)}) copy-start(f32[12,512]{1,0:T(8,128)} %get-tuple-element.17) | copy-start | bytes 73732

commit v2 on v1

--- a/solution.py
+++ b/solution.py
@@ -127,7 +127,7 @@
         e_across().start()
 
     def unit_slice(ref, u):
-        return ref.at[:, u // 2, pl.ds(pl.multiple_of((u % 2) * half, half), half), :]
+        return ref.at[:, u // 2, :, pl.ds(pl.multiple_of((u % 2) * half, half), half)]
 
     def unit_in(u):
         return pltpu.make_async_copy(unit_slice(mt, u), min_.at[u % 2], insem.at[u % 2])
@@ -209,24 +209,24 @@
             product = jnp.dot(lzb[...], first, preferred_element_type=f32)
             second = (ubuf[1, m].astype(f32) - product).astype(bf16)
             ucat[size:, :] = jnp.where(block_col > 1, second, zero)
-            csum[...] = jnp.zeros_like(csum)
-
+
+        csum[...] = jnp.zeros_like(csum)
         unit_in(u).wait()
 
         @pl.when(u >= 2)
         def _():
             unit_out(u - 2).wait()
 
-        rows = pl.ds(pl.multiple_of(h * half, half), half)
-
-        @pl.loop(0, row_blocks)
+        cols = pl.ds(pl.multiple_of(h * half, half), half)
+
+        @pl.loop(0, row_blocks, unroll=True)
         def _(a):
-            product = jnp.dot(lcat[a, rows, :], ucat[...], preferred_element_type=f32)
+            product = jnp.dot(lcat[a], ucat[:, cols], preferred_element_type=f32)
             result = min_[slot, a].astype(f32) - product
             mout[slot, a] = result.astype(bf16)
-            weight = gcol[a, rows, :]
-            weight = jnp.concatenate([weight] * (size // 128), axis=1)
-            csum[...] += jnp.sum((weight * result).reshape(half // 8, 8, size), axis=0)
+            weight = gcol[a]
+            weight = jnp.concatenate([weight] * (half // 128), axis=1)
+            csum[...] += jnp.sum((weight * result).reshape(size // 8, 8, half), axis=0)
 
         for band in range(2):
             @pl.when(block_col == band)
@@ -235,7 +235,8 @@
                 def _(a):
                     @pl.when(a * grid_rows + me_r > band)
                     def _():
-                        mout[slot, a] = lcat[a, rows, band * size:(band + 1) * size]
+                        from_col = pl.multiple_of(band * size + h * half, half)
+                        mout[slot, a] = lcat[a, :, pl.ds(from_col, half)]
 
         unit_out(u).start()
 
@@ -243,9 +244,7 @@
         def _():
             unit_in(u + 2).start()
 
-        @pl.when(h == 1)
-        def _():
-            crow[pl.ds(m, 1), :] = jnp.sum(csum[...], axis=0, keepdims=True)
+        crow[pl.ds(m, 1), cols] = jnp.sum(csum[...], axis=0, keepdims=True)
 
     @pl.loop(ahead, n_sub + 2)
     def _(t):
@@ -328,10 +327,10 @@
             pltpu.VMEM((2, 2, half, size), bf16),
             pltpu.VMEM((size, size), bf16),
             pltpu.VMEM((2 * size, size), bf16),
-            pltpu.VMEM((2, row_blocks, half, size), bf16),
-            pltpu.VMEM((2, row_blocks, half, size), bf16),
+            pltpu.VMEM((2, row_blocks, size, half), bf16),
+            pltpu.VMEM((2, row_blocks, size, half), bf16),
             pltpu.VMEM((row_blocks, size, 128), f32),
-            pltpu.VMEM((8, size), f32),
+            pltpu.VMEM((8, half), f32),
             pltpu.VMEM((col_blocks, size), f32),
             pltpu.VMEM((grid_rows, col_blocks, size), f32),
             dma((2, n_sub)), dma((n_sub,)), dma((n_sub,)),

time: 222 us -> 217 us (0.977)
  Pallas kernels: 194 us -> 188 us
    pallas_call x1, Pallas kernels: 194 us -> 188 us  [local(): pl.pallas_call(functools.partial(kernel, dims), out_shape=(jax.ShapeDtype...]
where the time goes in v2:
time: 217 us; the launch traced here: 216 us
  Pallas kernels  188 us (87%)
  local copies, waits for them, and re-layouts  27.4 us (13%)
    pallas_call x1, Pallas kernels, local(): pl.pallas_call(functools.partial(kernel, dims), out_shape=(jax.ShapeDtype...  188 us
    unnamed x5, local copies, waits for them, and re-layouts  27.4 us

profile of v2, /device:TPU:6, one launch (start us, length us, event | category | flops | bytes accessed | tf_op | source)
XLA Modules:
  0.0 216.0 jit_solution(1336956560921458348)
XLA Ops:
  0.6 188.0 %shard_map.58 = (bf16[6,12,512,512]{3,2,1,0:T(8,128)(2,1)}, f32[12,512]{1,0:T(8,128)}, f32[12,512]{1,0:T(8,128)}) custom-call(bf16[6,12,512,512]{3,2,1,0:T(8,128)(2,1)} %bitcast.3, bf16[2,512,512]{2,1,0:T(8,128)(2,1)} %mult.1, f32[6,512]{1,0:T(8,128)} %g.1), custom_call_target="tpu_custom_call" | custom-call | tf_op jit(solution)/shard_map/pallas_call | solution.py:314
  188.6 1.4 copy.6
  190.0 0.0 copy-start
  190.0 25.4 %copy.9 = bf16[6,512,12,512]{3,1,2,0:T(8,128)(2,1)} copy(bf16[6,512,12,512]{3,1,2,0:T(8,128)(2,1)} %bitcast.4) | data formatting | bytes 75497472
  215.4 0.0 copy-done
  215.4 0.6 copy.10
Async XLA Ops:
  190.0 25.4 %copy-start = (f32[12,512]{1,0:T(8,128)S(1)}, f32[12,512]{1,0:T(8,128)}, u32[]{:S(2)}) copy-start(f32[12,512]{1,0:T(8,128)} %get-tuple-element.17) | copy-start | bytes 73732
